TPU v7x, 32 devices: a whole 2x2x4 slice. The times are simulated.
32 devices in a mesh: frame: 8 (over y, x, core), module: 4 (over z).
Axes of the slice: x: 2, y: 2, z: 4, core: 2. Of those that a mesh axis runs over, the one named last changes fastest.
Arguments:
- raw_frames: int32 [2048, 32768], P('frame', 'module'), may hold values from 256 to 3856
- dark_frame: float32 [32768], P('module'), may hold values from 0 to 240
- flat_field: float32 [32768], P('module'), may hold values from 0.125 to 2.625, as said below
- membership: int32 [16, 32768], P(None, 'module'), may hold values from 0 to 1, as said below
Outputs:
- correlation: float32 [16, 8, 5, 256, 256], P('module', 'frame')
Inputs may be any that keep to these rules, and one draw needn't show every extreme that they name: `membership`: each pixel belongs to exactly one q-bin, and every module holds exactly 512 pixels of each q-bin, in no particular order. `flat_field`: positive gains.
All inputs are finite; a program needn't handle non-finite values.
Results may differ from a plain program's by a relative error of at most 0.0003.
Values may be sent and summed in bfloat16 or wider, within the bound.
A program may use at most 128 MiB of HBM per device.

v0:
```python
import functools

import jax
import jax.numpy as jnp
from jax import lax
from jax.experimental import pallas as pl
from jax.experimental.pallas import tpu as pltpu
from jax.sharding import PartitionSpec as P

MESH = pl.DeviceIdType.MESH
VMEM_BYTES = 60 * 1024 * 1024


def turn_kernel(raw, dark, flat, members, turned, sums):
    @pl.when(pl.program_id(0) == 0)
    def _():
        sums[...] = jnp.zeros_like(sums)

    intensity = (raw[...].astype(jnp.float32) - dark[...]) * flat[...]
    lines = intensity.T
    turned[...] = lines
    sums[...] += jnp.dot(
        members[...].astype(jnp.float32),
        lines,
        precision=lax.Precision.HIGHEST,
        preferred_element_type=jnp.float32,
    )


def turn(raw_frames, dark_frame, flat_field, membership):
    frames, pixels = raw_frames.shape
    bins = membership.shape[0]
    chunk = pixels // bins
    return pl.pallas_call(
        turn_kernel,
        out_shape=(
            jax.ShapeDtypeStruct((pixels, frames), jnp.float32),
            jax.ShapeDtypeStruct((bins, frames), jnp.float32),
        ),
        grid=(pixels // chunk,),
        in_specs=[
            pl.BlockSpec((frames, chunk), lambda i: (0, i)),
            pl.BlockSpec((1, chunk), lambda i: (0, i)),
            pl.BlockSpec((1, chunk), lambda i: (0, i)),
            pl.BlockSpec((bins, chunk), lambda i: (0, i)),
        ],
        out_specs=(
            pl.BlockSpec((chunk, frames), lambda i: (i, 0)),
            pl.BlockSpec((bins, frames), lambda i: (0, 0)),
        ),
    )(raw_frames, dark_frame[None, :], flat_field[None, :], membership)


def gram(left, right):
    return lax.dot_general(
        left, right, (((0,), (0,)), ((), ())), preferred_element_type=jnp.float32
    )


def correlate_kernel(
    blocks,
    modules,
    order,
    turned,
    sums,
    out,
    all_sums,
    scaled,
    own,
    far,
    near,
    hold,
    staged,
    sum_send,
    sum_recv,
    bin_send,
    bin_recv,
    frame_send,
    frame_recv,
    relay_send,
    relay_recv,
    result_send,
    result_recv,
):
    me = lax.axis_index("frame")
    module = lax.axis_index("module")
    pixels, frames = turned.shape
    bins = sums.shape[0]
    per_bin = pixels // bins
    owned = bins // modules
    even = lax.rem(me, 2) == 0
    odd = lax.rem(me, 2) == 1
    has_down = me >= 2
    has_up = me + 2 < blocks
    mate = me + 1 - 2 * lax.rem(me, 2)
    relayed = blocks == 8
    across = lax.rem(me + 4, 8)
    relaying = (me < 2) | (me >= 6)
    relay_parity = jnp.where(me >= 6, 1 - lax.rem(me, 2), lax.rem(me, 2))
    relay_target = jnp.where(even, 2, 5)

    barrier = pltpu.get_barrier_semaphore()

    def greet(frame, mod):
        pl.semaphore_signal(barrier, inc=1, device_id=(frame, mod), device_id_type=MESH)

    for gap in range(1, modules):
        greet(me, lax.rem(module + gap, modules))
    greet(mate, module)
    if relayed:
        greet(across, module)

    @pl.when(has_down)
    def _():
        greet(me - 2, module)

    @pl.when(has_up)
    def _():
        greet(me + 2, module)

    peers = modules + int(relayed) + has_down.astype(jnp.int32) + has_up.astype(jnp.int32)
    pl.semaphore_wait(barrier, peers)

    def sum_copy(gap):
        return pltpu.make_async_remote_copy(
            src_ref=sums,
            dst_ref=all_sums.at[module],
            send_sem=sum_send.at[gap - 1],
            recv_sem=sum_recv.at[gap - 1],
            device_id=(me, lax.rem(module + gap, modules)),
            device_id_type=MESH,
        )

    for gap in range(1, modules):
        sum_copy(gap).start()
    all_sums[module] = sums[...]
    for gap in range(1, modules):
        sum_copy(gap).wait()
    total = all_sums[0]
    for source in range(1, modules):
        total = total + all_sums[source]
    all_sums[0] = jnp.sqrt(jnp.float32(per_bin * modules)) / total

    half = per_bin // 2
    parts = 2 * modules

    def bin_copy(k, piece):
        gap, part = piece // 2, lax.rem(piece, 2)
        owner = lax.rem(module + gap, modules)
        start = pl.multiple_of(part * half, half)
        landing = pl.multiple_of(module * per_bin + part * half, half)
        return pltpu.make_async_remote_copy(
            src_ref=scaled.at[owner * owned + k, pl.ds(start, half), :],
            dst_ref=own.at[k, pl.ds(landing, half), :],
            send_sem=bin_send.at[k, piece],
            recv_sem=bin_recv.at[k, piece],
            device_id=(me, owner),
            device_id_type=MESH,
        )

    row_index = lax.broadcasted_iota(jnp.int32, (8, frames), 0)

    def fill(label, target, first):
        factor = all_sums[0, pl.ds(label, 1), :]

        def tile(start):
            lines = jnp.broadcast_to(turned[pl.ds(order[start], 1), :], (8, frames))
            for row in range(1, 8):
                line = turned[pl.ds(order[start + row], 1), :]
                lines = jnp.where(row_index == row, line, lines)
            return lines * factor

        def tiles(group, carry):
            start = label * per_bin + group * 16
            both = jnp.concatenate([tile(start), tile(start + 8)], axis=0)
            rows = pl.ds(pl.multiple_of(first + group * 16, 16), 16)
            target[rows, :] = both.astype(jnp.bfloat16)
            return carry

        lax.fori_loop(0, per_bin // 16, tiles, 0, unroll=4)

    def rows_of(j):
        source = lax.rem(module + modules - j // 2, modules)
        return pl.ds(pl.multiple_of(source * per_bin + lax.rem(j, 2) * half, half), half)

    def frame_copy(k, j, slot, target, frame):
        return pltpu.make_async_remote_copy(
            src_ref=own.at[k, rows_of(j), :],
            dst_ref=target.at[k, rows_of(j), :],
            send_sem=frame_send.at[slot, k, j],
            recv_sem=frame_recv.at[slot, k, j],
            device_id=(frame, module),
            device_id_type=MESH,
        )

    def far_copy(k, j):
        return frame_copy(k, j, 0, far, jnp.where(even, me - 2, me + 2))

    def mate_copy(k, j):
        return frame_copy(k, j, 1, near, mate)

    def entry_copy(k, j):
        straight = jnp.where(even, me + 2, me - 2)
        return pltpu.make_async_remote_copy(
            src_ref=own.at[k, rows_of(j), :],
            dst_ref=hold.at[k, rows_of(j), :],
            send_sem=frame_send.at[0, k, j],
            recv_sem=relay_recv.at[k, j],
            device_id=(jnp.where(lax.rem(k, 2) == 0, across, straight), module),
            device_id_type=MESH,
        )

    def exit_copy(k, j):
        return pltpu.make_async_remote_copy(
            src_ref=hold.at[k, rows_of(j), :],
            dst_ref=far.at[k, rows_of(j), :],
            send_sem=relay_send.at[k, j],
            recv_sem=frame_recv.at[0, k, j],
            device_id=(relay_target, module),
            device_id_type=MESH,
        )

    sends_far = (even & has_down) | (odd & has_up)
    diagonal = ((me == 3) | (me == 4)) if relayed else None

    def result_copy(k, stage, place, frame):
        return pltpu.make_async_remote_copy(
            src_ref=staged.at[stage, k],
            dst_ref=out.at[k, place],
            send_sem=result_send.at[stage, k],
            recv_sem=result_recv.at[place, k],
            device_id=(frame, module),
            device_id_type=MESH,
        )

    def pass_on(k, j):
        @pl.when(odd)
        def _():
            mate_copy(k, j).start()

        if relayed:
            @pl.when(diagonal)
            def _():
                entry_copy(k, j).start()

            @pl.when(sends_far & jnp.logical_not(diagonal))
            def _():
                far_copy(k, j).start()
        else:
            @pl.when(sends_far)
            def _():
                far_copy(k, j).start()

    def relay(k, j):
        if relayed:
            @pl.when(relaying & (lax.rem(k, 2) == relay_parity))
            def _():
                entry_copy(k, j).wait_recv()
                exit_copy(k, j).start()

    def await_frames(k, copy):
        for j in range(parts):
            copy(k, j).wait_recv()

    def correlate(k):
        out[k, 2] = gram(own[k], own[k])

        @pl.when(even)
        def _():
            await_frames(k, mate_copy)
            staged[0, k] = gram(near[k], own[k])
            result_copy(k, 0, 1, me + 1).start()
            out[k, 3] = gram(own[k], near[k])

        @pl.when(even & has_up)
        def _():
            await_frames(k, far_copy)
            staged[1, k] = gram(far[k], own[k])
            result_copy(k, 1, 0, me + 2).start()
            staged[2, k] = gram(far[k], near[k])
            result_copy(k, 2, 1, me + 2).start()
            staged[3, k] = gram(near[k], far[k])
            result_copy(k, 3, 3, me + 1).start()
            out[k, 4] = gram(own[k], far[k])

        @pl.when(odd & has_down)
        def _():
            await_frames(k, far_copy)
            staged[0, k] = gram(far[k], own[k])
            result_copy(k, 0, 4, me - 2).start()
            out[k, 0] = gram(own[k], far[k])

    @pl.loop(0, owned)
    def _(k):
        @pl.loop(1, modules)
        def _(gap):
            label = lax.rem(module + gap, modules) * owned + k
            fill(label, scaled.at[label], 0)
            bin_copy(k, 2 * gap).start()
            bin_copy(k, 2 * gap + 1).start()

        fill(module * owned + k, own.at[k], module * per_bin)
        pass_on(k, 0)
        pass_on(k, 1)

    @pl.loop(0, owned)
    def _(k):
        relay(k, 0)
        relay(k, 1)

    def receive(k, gaps):
        pieces = [2 * gap + part for gap in gaps for part in range(2)]
        for index, piece in enumerate(pieces):
            bin_copy(k, piece).wait()
            pass_on(k, piece)
            if index:
                relay(k, pieces[index - 1])
        relay(k, pieces[-1])

    @pl.loop(0, owned + 1)
    def _(turn_index):
        @pl.when(turn_index < owned)
        def _():
            receive(turn_index, range(1, modules))

        @pl.when(turn_index >= 1)
        def _():
            correlate(turn_index - 1)

    @pl.when(me < 2)
    def _():
        out[:, 0] = jnp.zeros_like(out[:, 0])

    @pl.when(me < 1)
    def _():
        out[:, 1] = jnp.zeros_like(out[:, 1])

    @pl.when(me + 1 >= blocks)
    def _():
        out[:, 3] = jnp.zeros_like(out[:, 3])

    @pl.when(me + 2 >= blocks)
    def _():
        out[:, 4] = jnp.zeros_like(out[:, 4])

    @pl.loop(0, owned)
    def _(k):
        @pl.when(even & has_down)
        def _():
            result_copy(k, 1, 0, me).wait_recv()
            result_copy(k, 2, 1, me).wait_recv()

        @pl.when(odd)
        def _():
            for j in range(parts):
                mate_copy(k, j).wait_send()
            result_copy(k, 0, 1, me).wait_recv()

        @pl.when(sends_far)
        def _():
            for j in range(parts):
                far_copy(k, j).wait_send()

        @pl.when(odd & has_up)
        def _():
            result_copy(k, 3, 3, me).wait_recv()
            result_copy(k, 0, 4, me).wait_recv()

        if relayed:
            @pl.when(relaying & (lax.rem(k, 2) == relay_parity))
            def _():
                for j in range(parts):
                    exit_copy(k, j).wait_send()

        @pl.when(even)
        def _():
            result_copy(k, 0, 1, me + 1).wait_send()

        @pl.when(even & has_up)
        def _():
            result_copy(k, 1, 0, me + 2).wait_send()
            result_copy(k, 2, 1, me + 2).wait_send()
            result_copy(k, 3, 3, me + 1).wait_send()

        @pl.when(odd & has_down)
        def _():
            result_copy(k, 0, 4, me - 2).wait_send()


def correlate(order, turned, sums):
    (pixels, frames), bins = turned.shape, sums.shape[0]
    per_bin = pixels // bins
    blocks, modules = lax.axis_size("frame"), lax.axis_size("module")
    owned = bins // modules
    gathered = per_bin * modules
    vmem = pl.BlockSpec(memory_space=pltpu.VMEM)
    dma = pltpu.SemaphoreType.DMA
    return pl.pallas_call(
        functools.partial(correlate_kernel, blocks, modules),
        out_shape=jax.ShapeDtypeStruct((owned, 5, frames, frames), jnp.float32),
        in_specs=[pl.BlockSpec(memory_space=pltpu.SMEM), vmem, vmem],
        out_specs=vmem,
        scratch_shapes=[
            pltpu.VMEM((modules, bins, frames), jnp.float32),
            pltpu.VMEM((bins, per_bin, frames), jnp.bfloat16),
            pltpu.VMEM((owned, gathered, frames), jnp.bfloat16),
            pltpu.VMEM((owned, gathered, frames), jnp.bfloat16),
            pltpu.VMEM((owned, gathered, frames), jnp.bfloat16),
            pltpu.VMEM((owned, gathered, frames), jnp.bfloat16),
            pltpu.VMEM((4, owned, frames, frames), jnp.float32),
            dma((modules - 1,)),
            dma((modules - 1,)),
            dma((owned, 2 * modules)),
            dma((owned, 2 * modules)),
            dma((2, owned, 2 * modules)),
            dma((2, owned, 2 * modules)),
            dma((owned, 2 * modules)),
            dma((owned, 2 * modules)),
            dma((4, owned)),
            dma((5, owned)),
        ],
        compiler_params=pltpu.CompilerParams(
            collective_id=0, has_side_effects=True, vmem_limit_bytes=VMEM_BYTES
        ),
    )(order, turned, sums)


def per_device(raw_frames, dark_frame, flat_field, membership):
    bins, pixels = membership.shape
    labels = jnp.sum(membership * jnp.arange(bins, dtype=jnp.int32)[:, None], axis=0)
    place = jnp.arange(pixels, dtype=jnp.int32)
    keys = jnp.sort(labels * pixels + place)
    order = keys - place // (pixels // bins) * pixels
    turned, sums = turn(raw_frames, dark_frame, flat_field, membership)
    return correlate(order, turned, sums)[:, None]


def solution(mesh):
    in_specs = (P("frame", "module"), P("module"), P("module"), P(None, "module"))
    out_specs = P("module", "frame", None, None, None)
    return jax.shard_map(
        per_device, mesh=mesh, in_specs=in_specs, out_specs=out_specs, check_vma=False
    )
```

profile of v0, /device:TPU:12, one launch (start us, length us, event | category | flops | bytes accessed | tf_op | source)
XLA Modules:
  0.0 179.6 jit_solution(9637067017618790883)
XLA Ops:
  0.0 1.1 multiply_reduce_fusion
  1.2 6.8 %sort.15 = (s32[8192]{0:T(1024)S(1)}, s32[8192]{0:T(1024)}) sort(s32[8192]{0:T(1024)S(1)} %iota_add_fusion, s32[8192]{0:T(1024)S(1)} %iota.13), dimensions={0}, to_apply=%region_1.0 | sort | flops 106496 | bytes 131072 | tf_op jit(solution)/shard_map/jit(sort)/sort | solution.py:432
  7.9 0.6 fusion.1.order
  8.6 13.9 %shard_map.46 = (f32[8192,256]{1,0:T(8,128)}, f32[16,256]{1,0:T(8,128)}) custom-call(s32[256,8192]{1,0:T(8,128)} %raw.1, f32[1,8192]{1,0:T(1,128)} %bitcast.6, f32[1,8192]{1,0:T(1,128)} %bitcast.7, s32[16,8192]{1,0:T(8,128)} %members.1), custom_call_target="tpu_custom_call" | custom-call | tf_op jit(solution)/shard_map/pallas_call | solution.py:34
  22.5 151.8 %shard_map.47 = f32[4,5,256,256]{3,2,1,0:T(8,128)} custom-call(s32[8192]{0:T(1024)} %fusion.1.order, f32[8192,256]{1,0:T(8,128)} %get-tuple-element.10.turned, f32[16,256]{1,0:T(8,128)} %get-tuple-element.11.sums), custom_call_target="tpu_custom_call" | custom-call | tf_op jit(solution)/shard_map/pallas_call | solution.py:398
  174.2 5.3 %copy.7 = f32[4,1,5,256,256]{4,3,2,1,0:T(8,128)} copy(f32[4,1,5,256,256]{4,3,2,1,0:T(8,128)} %bitcast.5) | data formatting | bytes 10485760
  (2 shorter events, 0.0 us)
where the time goes:
time: 180 us
  Pallas kernels  166 us (92%)
  other arithmetic  8.54 us (5%)
  local copies, waits for them, and re-layouts  5.32 us (3%)
    pallas_call x1, Pallas kernels, correlate(): pl.pallas_call(functools.partial(correlate_kernel, blocks, modules), out_...  152 us
    pallas_call x1, Pallas kernels, turn(): pl.pallas_call(turn_kernel, out_shape=(jax.ShapeDtypeStruct((pixels, fram...  13.9 us
    sort x1, other arithmetic, per_device(): keys = jnp.sort(labels * pixels + place)  6.77 us
    unnamed x1, local copies, waits for them, and re-layouts  5.32 us

commit v1 on v0

--- a/solution.py
+++ b/solution.py
@@ -9,6 +9,49 @@
 
 MESH = pl.DeviceIdType.MESH
 VMEM_BYTES = 60 * 1024 * 1024
+LANES = 128
+
+
+def order_kernel(members, order):
+    bins, pixels = members.shape
+    per_bin = pixels // bins
+    span = 2 * LANES
+    rows = pixels // LANES
+    f32, bf16 = jnp.float32, jnp.bfloat16
+    upto = lax.broadcasted_iota(jnp.int32, (span, span), 0)
+    upto = (upto <= lax.broadcasted_iota(jnp.int32, (span, span), 1)).astype(f32).astype(bf16)
+    base = lax.broadcasted_iota(jnp.int32, (bins, span), 0).astype(f32) * per_bin - 1.0
+    row_of = lax.broadcasted_iota(jnp.int32, (rows, span), 0)
+    lane_of = lax.broadcasted_iota(jnp.int32, (LANES, span), 0)
+    place = lax.broadcasted_iota(jnp.int32, (rows, span), 1).astype(f32)
+    high = jnp.zeros((rows, LANES), f32)
+    low = jnp.zeros((rows, LANES), f32)
+    for chunk in range(pixels // span):
+        one_hot = members[:, chunk * span : (chunk + 1) * span].astype(f32)
+        seen = jnp.dot(one_hot.astype(bf16), upto, preferred_element_type=f32)
+        slot = jnp.sum(one_hot * (seen + base), axis=0, keepdims=True).astype(jnp.int32)
+        base = base + jnp.sum(one_hot, axis=1, keepdims=True)
+        in_row = row_of == jnp.broadcast_to(slot // LANES, (rows, span))
+        in_lane = lane_of == jnp.broadcast_to(slot % LANES, (LANES, span))
+        in_lane = in_lane.astype(f32).astype(bf16)
+        lows = jnp.where(in_row, place, 0.0).astype(bf16)
+        highs = jnp.where(in_row, float(chunk), 0.0).astype(bf16)
+        both = (((1,), (1,)), ((), ()))
+        low += lax.dot_general(lows, in_lane, both, preferred_element_type=f32)
+        high += lax.dot_general(highs, in_lane, both, preferred_element_type=f32)
+    order[...] = (high * span + low).astype(jnp.int32)
+
+
+def pixel_order(membership):
+    pixels = membership.shape[1]
+    vmem = pl.BlockSpec(memory_space=pltpu.VMEM)
+    table = pl.pallas_call(
+        order_kernel,
+        out_shape=jax.ShapeDtypeStruct((pixels // LANES, LANES), jnp.int32),
+        in_specs=[vmem],
+        out_specs=vmem,
+    )(membership)
+    return table.reshape(pixels)
 
 
 def turn_kernel(raw, dark, flat, members, turned, sums):
@@ -57,7 +100,7 @@
     )
 
 
-def correlate_kernel(
+def chain_kernel(
     blocks,
     modules,
     order,
@@ -387,7 +430,7 @@
             result_copy(k, 0, 4, me - 2).wait_send()
 
 
-def correlate(order, turned, sums):
+def correlate_chain(order, turned, sums):
     (pixels, frames), bins = turned.shape, sums.shape[0]
     per_bin = pixels // bins
     blocks, modules = lax.axis_size("frame"), lax.axis_size("module")
@@ -396,7 +439,7 @@
     vmem = pl.BlockSpec(memory_space=pltpu.VMEM)
     dma = pltpu.SemaphoreType.DMA
     return pl.pallas_call(
-        functools.partial(correlate_kernel, blocks, modules),
+        functools.partial(chain_kernel, blocks, modules),
         out_shape=jax.ShapeDtypeStruct((owned, 5, frames, frames), jnp.float32),
         in_specs=[pl.BlockSpec(memory_space=pltpu.SMEM), vmem, vmem],
         out_specs=vmem,
@@ -425,14 +468,390 @@
     )(order, turned, sums)
 
 
+def square_kernel(
+    modules,
+    order,
+    raw,
+    dark,
+    flat,
+    out,
+    counts_in,
+    turned,
+    packed,
+    own,
+    near,
+    first,
+    second,
+    third,
+    staged,
+    raw_sem,
+    bin_send,
+    bin_recv,
+    frame_send,
+    frame_recv,
+    result_send,
+    result_recv,
+):
+    me = lax.axis_index("frame")
+    module = lax.axis_index("module")
+    pixels, frames = turned.shape
+    bins = packed.shape[0]
+    per_bin = pixels // bins
+    owned = bins // modules
+    gathered = per_bin * modules
+    half = per_bin // 2
+    parts = 2 * modules
+
+    side = me // 4
+    sign = 1 - 2 * side
+
+    def flip(block):
+        return jnp.where(side == 1, 7 - block, block)
+
+    role = flip(me)
+    mate = me + 1 - 2 * lax.rem(me, 2)
+    is_one, is_two, is_three = role == 1, role == 2, role == 3
+
+    def place(gap):
+        return 2 + sign * gap
+
+    barrier = pltpu.get_barrier_semaphore()
+
+    def greet(frame, mod):
+        pl.semaphore_signal(barrier, inc=1, device_id=(frame, mod), device_id_type=MESH)
+
+    for gap in range(1, modules):
+        greet(me, lax.rem(module + gap, modules))
+    greet(mate, module)
+
+    @pl.when(is_one)
+    def _():
+        greet(flip(2), module)
+        greet(flip(3), module)
+        greet(flip(4), module)
+
+    @pl.when(is_two | is_three)
+    def _():
+        greet(flip(1), module)
+
+    @pl.when(is_three)
+    def _():
+        greet(flip(6), module)
+
+    slab = counts_in.shape[2]
+    slabs = pixels // slab
+
+    def load(index):
+        start = pl.multiple_of(index * slab, slab)
+        slot = lax.rem(index, 2)
+        return pltpu.make_async_copy(
+            raw.at[:, pl.ds(start, slab)], counts_in.at[slot], raw_sem.at[slot]
+        )
+
+    load(0).start()
+    load(1).start()
+
+    @pl.loop(0, slabs)
+    def _(index):
+        load(index).wait()
+        start = pl.multiple_of(index * slab, slab)
+        columns = pl.ds(start, slab)
+        raw_counts = counts_in[lax.rem(index, 2)].astype(jnp.float32)
+        turned[columns, :] = ((raw_counts - dark[:, columns]) * flat[:, columns]).T
+
+        @pl.when(index + 2 < slabs)
+        def _():
+            load(index + 2).start()
+
+    peers = modules + jnp.where(is_one, 3, jnp.where(is_three, 2, jnp.where(is_two, 1, 0)))
+    pl.semaphore_wait(barrier, peers)
+
+    row_index = lax.broadcasted_iota(jnp.int32, (8, frames), 0)
+
+    def fill(label, target, first_row):
+        def tile(start):
+            lines = jnp.broadcast_to(turned[pl.ds(order[start], 1), :], (8, frames))
+            for row in range(1, 8):
+                line = turned[pl.ds(order[start + row], 1), :]
+                lines = jnp.where(row_index == row, line, lines)
+            return lines
+
+        def tiles(group, carry):
+            start = label * per_bin + group * 16
+            both = jnp.concatenate([tile(start), tile(start + 8)], axis=0)
+            rows = pl.ds(pl.multiple_of(first_row + group * 16, 16), 16)
+            target[rows, :] = both.astype(jnp.bfloat16)
+            return carry
+
+        lax.fori_loop(0, per_bin // 16, tiles, 0, unroll=4)
+
+    def bin_copy(k, piece):
+        gap, part = piece // 2, lax.rem(piece, 2)
+        owner = lax.rem(module + gap, modules)
+        start = pl.multiple_of(part * half, half)
+        landing = pl.multiple_of(module * per_bin + part * half, half)
+        return pltpu.make_async_remote_copy(
+            src_ref=packed.at[owner * owned + k, pl.ds(start, half), :],
+            dst_ref=own.at[k, pl.ds(landing, half), :],
+            send_sem=bin_send.at[k, piece],
+            recv_sem=bin_recv.at[k, piece],
+            device_id=(me, owner),
+            device_id_type=MESH,
+        )
+
+    def rows_of(j):
+        source = lax.rem(module + modules - j // 2, modules)
+        return pl.ds(pl.multiple_of(source * per_bin + lax.rem(j, 2) * half, half), half)
+
+    def frame_copy(flow, k, j, target, frame):
+        return pltpu.make_async_remote_copy(
+            src_ref=own.at[k, rows_of(j), :],
+            dst_ref=target.at[rows_of(j), :],
+            send_sem=frame_send.at[flow, k, j],
+            recv_sem=frame_recv.at[flow, k, j],
+            device_id=(frame, module),
+            device_id_type=MESH,
+        )
+
+    def near_copy(k, j):
+        return frame_copy(0, k, j, near.at[k], mate)
+
+    def first_copy(k, j):
+        return frame_copy(1, k, j, first.at[k], jnp.where(is_one, flip(3), flip(1)))
+
+    def second_copy(k, j):
+        return frame_copy(2, k, j, second.at[k], flip(6))
+
+    def third_copy(k, j):
+        return frame_copy(3, k, j, third.at[k // 2], flip(1))
+
+    def shared(k):
+        return lax.rem(k, 2) == side
+
+    def pass_on(k, j):
+        @pl.when(is_one | is_two)
+        def _():
+            first_copy(k, j).start()
+
+        @pl.when(is_three)
+        def _():
+            second_copy(k, j).start()
+
+        @pl.when(is_three & shared(k))
+        def _():
+            third_copy(k, j).start()
+
+        near_copy(k, j).start()
+
+    def result_copy(k, stage, spot, frame):
+        return pltpu.make_async_remote_copy(
+            src_ref=staged.at[stage, k],
+            dst_ref=out.at[k, spot],
+            send_sem=result_send.at[stage, k],
+            recv_sem=result_recv.at[spot, k],
+            device_id=(frame, module),
+            device_id_type=MESH,
+        )
+
+    one_results = ((2, 0), (2, 4), (4, 2), (0, 2), (3, 4), (4, 3))
+    three_results = ((1, 3), (2, 1))
+
+    def result_of(k, stage, pair):
+        return result_copy(k, stage, place(pair[1] - pair[0]), flip(pair[0]))
+
+    def scale_of(block):
+        down = jnp.ones((8, gathered), jnp.bfloat16)
+        across = jnp.ones((gathered, LANES), jnp.bfloat16)
+        root = jnp.sqrt(jnp.float32(gathered))
+        row = jnp.dot(down, block, preferred_element_type=jnp.float32)[:1]
+        column = gram(block, across)
+        column = jnp.concatenate([column] * (frames // LANES), axis=1)
+        return root / column, root / row
+
+    def await_frames(k, copy):
+        for j in range(parts):
+            copy(k, j).wait_recv()
+
+    def correlate(k):
+        scales = {0: scale_of(own[k])}
+        out[k, 2] = gram(own[k], own[k]) * scales[0][0] * scales[0][1]
+        await_frames(k, near_copy)
+        near_scale = scale_of(near[k])
+        own_scale = scales[0]
+        out[k, mate - me + 2] = gram(own[k], near[k]) * own_scale[0] * near_scale[1]
+
+        @pl.when(is_three)
+        def _():
+            await_frames(k, first_copy)
+            scale = scale_of(first[k])
+            staged[0, k] = gram(first[k], own[k]) * scale[0] * own_scale[1]
+            result_of(k, 0, three_results[0]).start()
+            staged[1, k] = gram(near[k], first[k]) * near_scale[0] * scale[1]
+            result_of(k, 1, three_results[1]).start()
+            out[k, place(-2)] = gram(own[k], first[k]) * own_scale[0] * scale[1]
+
+        @pl.when(is_one)
+        def _():
+            await_frames(k, first_copy)
+            scale = scale_of(first[k])
+            staged[0, k] = gram(first[k], near[k]) * scale[0] * near_scale[1]
+            result_of(k, 0, one_results[0]).start()
+            await_frames(k, second_copy)
+            far_scale = scale_of(second[k])
+            staged[1, k] = gram(first[k], second[k]) * scale[0] * far_scale[1]
+            result_of(k, 1, one_results[1]).start()
+            staged[2, k] = gram(second[k], first[k]) * far_scale[0] * scale[1]
+            result_of(k, 2, one_results[2]).start()
+
+            @pl.when(shared(k))
+            def _():
+                await_frames(k, third_copy)
+                block = third.at[k // 2]
+                third_scale = scale_of(block[...])
+                staged[4, k] = gram(block[...], second[k]) * third_scale[0] * far_scale[1]
+                result_of(k, 4, one_results[4]).start()
+                staged[5, k] = gram(second[k], block[...]) * far_scale[0] * third_scale[1]
+                result_of(k, 5, one_results[5]).start()
+
+            staged[3, k] = gram(near[k], first[k]) * near_scale[0] * scale[1]
+            result_of(k, 3, one_results[3]).start()
+            out[k, place(1)] = gram(own[k], first[k]) * own_scale[0] * scale[1]
+
+    @pl.loop(0, owned)
+    def _(k):
+        @pl.loop(1, modules)
+        def _(gap):
+            label = lax.rem(module + gap, modules) * owned + k
+            fill(label, packed.at[label], 0)
+            bin_copy(k, 2 * gap).start()
+            bin_copy(k, 2 * gap + 1).start()
+
+        fill(module * owned + k, own.at[k], module * per_bin)
+        pass_on(k, 0)
+        pass_on(k, 1)
+
+    @pl.when(role == 0)
+    def _():
+        for k in range(owned):
+            out[k, place(-1)] = jnp.zeros((frames, frames), jnp.float32)
+
+    @pl.when(role < 2)
+    def _():
+        for k in range(owned):
+            out[k, place(-2)] = jnp.zeros((frames, frames), jnp.float32)
+
+    @pl.loop(0, owned + 1)
+    def _(turn_index):
+        @pl.when(turn_index < owned)
+        def _():
+            for piece in range(2, parts):
+                bin_copy(turn_index, piece).wait()
+                pass_on(turn_index, piece)
+
+        @pl.when(turn_index >= 1)
+        def _():
+            correlate(turn_index - 1)
+
+    @pl.loop(0, owned)
+    def _(k):
+        for j in range(parts):
+            near_copy(k, j).wait_send()
+
+        @pl.when(is_one | is_two)
+        def _():
+            for j in range(parts):
+                first_copy(k, j).wait_send()
+
+        @pl.when(is_three)
+        def _():
+            for j in range(parts):
+                second_copy(k, j).wait_send()
+
+        @pl.when(is_three & shared(k))
+        def _():
+            for j in range(parts):
+                third_copy(k, j).wait_send()
+
+        @pl.when(is_one)
+        def _():
+            for stage in range(4):
+                result_of(k, stage, one_results[stage]).wait_send()
+
+        @pl.when(is_one & shared(k))
+        def _():
+            for stage in range(4, 6):
+                result_of(k, stage, one_results[stage]).wait_send()
+
+        @pl.when(is_three)
+        def _():
+            for stage in range(2):
+                result_of(k, stage, three_results[stage]).wait_send()
+
+        result_copy(k, 0, place(2), me).wait_recv()
+
+        @pl.when(is_two)
+        def _():
+            result_copy(k, 0, place(-2), me).wait_recv()
+            result_copy(k, 0, place(-1), me).wait_recv()
+
+        @pl.when(is_three)
+        def _():
+            result_copy(k, 0, place(1), me).wait_recv()
+
+
+def correlate_square(order, raw_frames, dark_frame, flat_field, bins):
+    frames, pixels = raw_frames.shape
+    modules = lax.axis_size("module")
+    per_bin = pixels // bins
+    owned = bins // modules
+    gathered = per_bin * modules
+    slab = 2 * per_bin
+    vmem = pl.BlockSpec(memory_space=pltpu.VMEM)
+    dma = pltpu.SemaphoreType.DMA
+    block = (owned, gathered, frames)
+    return pl.pallas_call(
+        functools.partial(square_kernel, modules),
+        out_shape=jax.ShapeDtypeStruct((owned, 5, frames, frames), jnp.float32),
+        in_specs=[
+            pl.BlockSpec(memory_space=pltpu.SMEM),
+            pl.BlockSpec(memory_space=pl.ANY),
+            vmem,
+            vmem,
+        ],
+        out_specs=vmem,
+        scratch_shapes=[
+            pltpu.VMEM((2, frames, slab), jnp.int32),
+            pltpu.VMEM((pixels, frames), jnp.float32),
+            pltpu.VMEM((bins, per_bin, frames), jnp.bfloat16),
+            pltpu.VMEM(block, jnp.bfloat16),
+            pltpu.VMEM(block, jnp.bfloat16),
+            pltpu.VMEM(block, jnp.bfloat16),
+            pltpu.VMEM(block, jnp.bfloat16),
+            pltpu.VMEM((owned // 2, gathered, frames), jnp.bfloat16),
+            pltpu.VMEM((6, owned, frames, frames), jnp.float32),
+            dma((2,)),
+            dma((owned, 2 * modules)),
+            dma((owned, 2 * modules)),
+            dma((4, owned, 2 * modules)),
+            dma((4, owned, 2 * modules)),
+            dma((6, owned)),
+            dma((5, owned)),
+        ],
+        compiler_params=pltpu.CompilerParams(
+            collective_id=1, has_side_effects=True, vmem_limit_bytes=VMEM_BYTES
+        ),
+    )(order, raw_frames, dark_frame[None, :], flat_field[None, :])
+
+
 def per_device(raw_frames, dark_frame, flat_field, membership):
-    bins, pixels = membership.shape
-    labels = jnp.sum(membership * jnp.arange(bins, dtype=jnp.int32)[:, None], axis=0)
-    place = jnp.arange(pixels, dtype=jnp.int32)
-    keys = jnp.sort(labels * pixels + place)
-    order = keys - place // (pixels // bins) * pixels
-    turned, sums = turn(raw_frames, dark_frame, flat_field, membership)
-    return correlate(order, turned, sums)[:, None]
+    order = pixel_order(membership)
+    if lax.axis_size("frame") == 8:
+        bins = membership.shape[0]
+        result = correlate_square(order, raw_frames, dark_frame, flat_field, bins)
+    else:
+        turned, sums = turn(raw_frames, dark_frame, flat_field, membership)
+        result = correlate_chain(order, turned, sums)
+    return result[:, None]
 
 
 def solution(mesh):

time: 180 us -> 149 us (0.83)
  Pallas kernels: 166 us -> 143 us
  other arithmetic: 8.54 us -> 0 us
    pallas_call x2, Pallas kernels: 166 us -> 143 us  [the longest x1 137 us: correlate_square(): pl.pallas_call(functools.partial(square_kernel, modules), out_shape=jax.S...]
    sort x1 -> x0, other arithmetic: 6.77 us -> none  [per_device(): keys = jnp.sort(labels * pixels + place)]
where the time goes in v1:
time: 149 us; the launch traced here: 148 us
  Pallas kernels  143 us (96%)
  local copies, waits for them, and re-layouts  5.32 us (4%)
    pallas_call x1, Pallas kernels, correlate_square(): pl.pallas_call(functools.partial(square_kernel, modules), out_shape=jax.S...  137 us
    pallas_call x1, Pallas kernels, pixel_order(): pl.pallas_call(order_kernel, out_shape=jax.ShapeDtypeStruct((pixels // LA...  6.09 us
    unnamed x1, local copies, waits for them, and re-layouts  5.32 us

profile of v1, /device:TPU:12, one launch (start us, length us, event | category | flops | bytes accessed | tf_op | source)
XLA Modules:
  0.0 148.3 jit_solution(4965619897160395673)
XLA Ops:
  0.0 6.1 %shard_map.46 = s32[64,128]{1,0:T(8,128)} custom-call(s32[16,8192]{1,0:T(8,128)} %members.1), custom_call_target="tpu_custom_call" | custom-call | tf_op jit(solution)/shard_map/pallas_call | solution.py:48
  6.1 136.9 %shard_map.47 = f32[4,5,256,256]{3,2,1,0:T(8,128)} custom-call(s32[8192]{0:T(1024)} %bitcast.7, s32[256,8192]{1,0:T(8,128)} %raw.1, f32[1,8192]{1,0:T(1,128)} %bitcast.8, f32[1,8192]{1,0:T(1,128)} %bitcast.9), custom_call_target="tpu_custom_call" | custom-call | tf_op jit(solution)/shard_map/pallas_call | solution.py:812
  143.0 5.3 %copy.7 = f32[4,1,5,256,256]{4,3,2,1,0:T(8,128)} copy(f32[4,1,5,256,256]{4,3,2,1,0:T(8,128)} %bitcast.6) | data formatting | bytes 10485760

commit v2 on v1

--- a/solution.py
+++ b/solution.py
@@ -9,37 +9,45 @@
 
 MESH = pl.DeviceIdType.MESH
 VMEM_BYTES = 60 * 1024 * 1024
+SQUARE_BYTES = 57 * 1024 * 1024
 LANES = 128
-
-
-def order_kernel(members, order):
+SEND_ORDER = ((3, 2, 1), (2, 3, 0), (1, 0, 3), (0, 1, 2))
+TAKE_ORDER = ((1, 3, 2), (0, 2, 3), (3, 1, 0), (2, 0, 1))
+
+
+def sort_pixels(members, lows_highs, lanes):
     bins, pixels = members.shape
     per_bin = pixels // bins
     span = 2 * LANES
     rows = pixels // LANES
     f32, bf16 = jnp.float32, jnp.bfloat16
-    upto = lax.broadcasted_iota(jnp.int32, (span, span), 0)
-    upto = (upto <= lax.broadcasted_iota(jnp.int32, (span, span), 1)).astype(f32).astype(bf16)
+    shape = (span, span + LANES)
+    upto = lax.broadcasted_iota(jnp.int32, shape, 0) <= lax.broadcasted_iota(jnp.int32, shape, 1)
+    upto = upto.astype(f32).astype(bf16)
     base = lax.broadcasted_iota(jnp.int32, (bins, span), 0).astype(f32) * per_bin - 1.0
     row_of = lax.broadcasted_iota(jnp.int32, (rows, span), 0)
     lane_of = lax.broadcasted_iota(jnp.int32, (LANES, span), 0)
     place = lax.broadcasted_iota(jnp.int32, (rows, span), 1).astype(f32)
-    high = jnp.zeros((rows, LANES), f32)
-    low = jnp.zeros((rows, LANES), f32)
     for chunk in range(pixels // span):
-        one_hot = members[:, chunk * span : (chunk + 1) * span].astype(f32)
+        columns = slice(chunk * span, (chunk + 1) * span)
+        one_hot = members[:, columns].astype(f32)
         seen = jnp.dot(one_hot.astype(bf16), upto, preferred_element_type=f32)
-        slot = jnp.sum(one_hot * (seen + base), axis=0, keepdims=True).astype(jnp.int32)
-        base = base + jnp.sum(one_hot, axis=1, keepdims=True)
+        slot = one_hot * (seen[:, :span] + base)
+        slot = jnp.sum(slot, axis=0, keepdims=True).astype(jnp.int32)
+        base = base + jnp.concatenate([seen[:, span:]] * 2, axis=1)
         in_row = row_of == jnp.broadcast_to(slot // LANES, (rows, span))
         in_lane = lane_of == jnp.broadcast_to(slot % LANES, (LANES, span))
-        in_lane = in_lane.astype(f32).astype(bf16)
-        lows = jnp.where(in_row, place, 0.0).astype(bf16)
-        highs = jnp.where(in_row, float(chunk), 0.0).astype(bf16)
-        both = (((1,), (1,)), ((), ()))
-        low += lax.dot_general(lows, in_lane, both, preferred_element_type=f32)
-        high += lax.dot_general(highs, in_lane, both, preferred_element_type=f32)
-    order[...] = (high * span + low).astype(jnp.int32)
+        lanes[:, columns] = in_lane.astype(f32).astype(bf16)
+        lows_highs[:rows, columns] = jnp.where(in_row, place, 0.0).astype(bf16)
+        lows_highs[rows:, columns] = jnp.where(in_row, float(chunk), 0.0).astype(bf16)
+    both = (((1,), (1,)), ((), ()))
+    table = lax.dot_general(lows_highs[...], lanes[...], both, preferred_element_type=f32)
+    table = (table[rows:] * span + table[:rows]).astype(jnp.int32)
+    return jnp.clip(table, 0, pixels - 1)
+
+
+def order_kernel(members, order, lows_highs, lanes):
+    order[...] = sort_pixels(members, lows_highs, lanes)
 
 
 def pixel_order(membership):
@@ -50,6 +58,10 @@
         out_shape=jax.ShapeDtypeStruct((pixels // LANES, LANES), jnp.int32),
         in_specs=[vmem],
         out_specs=vmem,
+        scratch_shapes=[
+            pltpu.VMEM((2 * pixels // LANES, pixels), jnp.bfloat16),
+            pltpu.VMEM((LANES, pixels), jnp.bfloat16),
+        ],
     )(membership)
     return table.reshape(pixels)
 
@@ -470,27 +482,45 @@
 
 def square_kernel(
     modules,
-    order,
     raw,
+    dark_frame,
+    flat_field,
+    membership,
+    total,
     dark,
     flat,
-    out,
+    members,
+    lows_highs,
+    lanes,
+    table,
+    order,
     counts_in,
     turned,
+    sums,
+    all_sums,
     packed,
     own,
     near,
     first,
     second,
     third,
-    staged,
+    direct,
+    coded,
+    coded_peak,
+    landed,
+    landed_peak,
     raw_sem,
+    order_sem,
+    sum_send,
+    sum_recv,
     bin_send,
     bin_recv,
     frame_send,
     frame_recv,
-    result_send,
-    result_recv,
+    direct_send,
+    direct_recv,
+    coded_send,
+    coded_recv,
 ):
     me = lax.axis_index("frame")
     module = lax.axis_index("module")
@@ -501,6 +531,12 @@
     gathered = per_bin * modules
     half = per_bin // 2
     parts = 2 * modules
+    f32, bf16 = jnp.float32, jnp.bfloat16
+
+    send_order, take_order = SEND_ORDER, TAKE_ORDER
+    if modules != 4:
+        send_order = [[(m + gap) % modules for gap in range(1, modules)] for m in range(modules)]
+        take_order = [[(m - gap) % modules for gap in range(1, modules)] for m in range(modules)]
 
     side = me // 4
     sign = 1 - 2 * side
@@ -538,52 +574,98 @@
     def _():
         greet(flip(6), module)
 
-    slab = counts_in.shape[2]
-    slabs = pixels // slab
+    slabs, _, slab = counts_in.shape
+
+    def columns_of(index):
+        return pl.ds(pl.multiple_of(index * slab, slab), slab)
 
     def load(index):
-        start = pl.multiple_of(index * slab, slab)
-        slot = lax.rem(index, 2)
         return pltpu.make_async_copy(
-            raw.at[:, pl.ds(start, slab)], counts_in.at[slot], raw_sem.at[slot]
-        )
-
-    load(0).start()
-    load(1).start()
+            raw.at[:, columns_of(index)], counts_in.at[index], raw_sem.at[index]
+        )
+
+    def intensity(index):
+        columns = columns_of(index)
+        return (counts_in[index].astype(f32) - dark[:, columns]) * flat[:, columns]
+
+    fetch = pltpu.make_async_copy(membership, members, order_sem.at[0])
+    fetch.start()
+    fetch_dark = pltpu.make_async_copy(dark_frame, dark, order_sem.at[2])
+    fetch_dark.start()
+    fetch_flat = pltpu.make_async_copy(flat_field, flat, order_sem.at[3])
+    fetch_flat.start()
+    sums[...] = jnp.zeros_like(sums)
+    fetch.wait()
+    for index in range(slabs):
+        load(index).start()
+    table[...] = sort_pixels(members, lows_highs, lanes)
+    spread = pltpu.make_async_copy(table, order, order_sem.at[1])
+    spread.start()
+    fetch_dark.wait()
+    fetch_flat.wait()
 
     @pl.loop(0, slabs)
     def _(index):
         load(index).wait()
-        start = pl.multiple_of(index * slab, slab)
-        columns = pl.ds(start, slab)
-        raw_counts = counts_in[lax.rem(index, 2)].astype(jnp.float32)
-        turned[columns, :] = ((raw_counts - dark[:, columns]) * flat[:, columns]).T
-
-        @pl.when(index + 2 < slabs)
-        def _():
-            load(index + 2).start()
+        values = intensity(index)
+        high = values.astype(bf16)
+        low = (values - high.astype(f32)).astype(bf16)
+        one_hot = members[:, columns_of(index)].astype(f32).astype(bf16)
+        both = (((1,), (1,)), ((), ()))
+        sums[...] += lax.dot_general(
+            one_hot, high, both, preferred_element_type=f32
+        ) + lax.dot_general(one_hot, low, both, preferred_element_type=f32)
 
     peers = modules + jnp.where(is_one, 3, jnp.where(is_three, 2, jnp.where(is_two, 1, 0)))
     pl.semaphore_wait(barrier, peers)
 
+    def sum_copy(gap):
+        return pltpu.make_async_remote_copy(
+            src_ref=sums,
+            dst_ref=all_sums.at[module],
+            send_sem=sum_send.at[gap - 1],
+            recv_sem=sum_recv.at[gap - 1],
+            device_id=(me, lax.rem(module + gap, modules)),
+            device_id_type=MESH,
+        )
+
+    for gap in range(1, modules):
+        sum_copy(gap).start()
+    all_sums[module] = sums[...]
+
+    @pl.loop(0, slabs)
+    def _(index):
+        turned[columns_of(index), :] = intensity(index).T
+
+    for gap in range(1, modules):
+        sum_copy(gap).wait()
+    bin_sums = all_sums[0]
+    for source in range(1, modules):
+        bin_sums = bin_sums + all_sums[source]
+    all_sums[0] = jnp.sqrt(f32(gathered)) / bin_sums
+
+    spread.wait()
     row_index = lax.broadcasted_iota(jnp.int32, (8, frames), 0)
 
-    def fill(label, target, first_row):
+    def fill(label, part, target, first_row):
+        factor = all_sums[0, pl.ds(label, 1), :]
+
         def tile(start):
-            lines = jnp.broadcast_to(turned[pl.ds(order[start], 1), :], (8, frames))
+            line, lane = start // LANES, lax.rem(start, LANES)
+            lines = jnp.broadcast_to(turned[pl.ds(order[line, lane], 1), :], (8, frames))
             for row in range(1, 8):
-                line = turned[pl.ds(order[start + row], 1), :]
-                lines = jnp.where(row_index == row, line, lines)
-            return lines
+                line_at = turned[pl.ds(order[line, lane + row], 1), :]
+                lines = jnp.where(row_index == row, line_at, lines)
+            return lines * factor
 
         def tiles(group, carry):
-            start = label * per_bin + group * 16
+            start = label * per_bin + part * half + group * 16
             both = jnp.concatenate([tile(start), tile(start + 8)], axis=0)
             rows = pl.ds(pl.multiple_of(first_row + group * 16, 16), 16)
-            target[rows, :] = both.astype(jnp.bfloat16)
+            target[rows, :] = both.astype(bf16)
             return carry
 
-        lax.fori_loop(0, per_bin // 16, tiles, 0, unroll=4)
+        lax.fori_loop(0, half // 16, tiles, 0, unroll=4)
 
     def bin_copy(k, piece):
         gap, part = piece // 2, lax.rem(piece, 2)
@@ -593,7 +675,7 @@
         return pltpu.make_async_remote_copy(
             src_ref=packed.at[owner * owned + k, pl.ds(start, half), :],
             dst_ref=own.at[k, pl.ds(landing, half), :],
-            send_sem=bin_send.at[k, piece],
+            send_sem=bin_send.at[0],
             recv_sem=bin_recv.at[k, piece],
             device_id=(me, owner),
             device_id_type=MESH,
@@ -607,8 +689,18 @@
         return pltpu.make_async_remote_copy(
             src_ref=own.at[k, rows_of(j), :],
             dst_ref=target.at[rows_of(j), :],
-            send_sem=frame_send.at[flow, k, j],
-            recv_sem=frame_recv.at[flow, k, j],
+            send_sem=frame_send.at[flow],
+            recv_sem=frame_recv.at[flow, k],
+            device_id=(frame, module),
+            device_id_type=MESH,
+        )
+
+    def whole_copy(flow, k, source, target, frame):
+        return pltpu.make_async_remote_copy(
+            src_ref=source,
+            dst_ref=target,
+            send_sem=frame_send.at[flow],
+            recv_sem=frame_recv.at[flow, k],
             device_id=(frame, module),
             device_id_type=MESH,
         )
@@ -643,164 +735,254 @@
 
         near_copy(k, j).start()
 
-    def result_copy(k, stage, spot, frame):
+    def pick(table, turn):
+        found = turn * 0
+        for row, others in enumerate(table):
+            for column, other in enumerate(others):
+                here = (module == row) & (turn == column)
+                found = jnp.where(here, (other - row) % modules, found)
+        return found
+
+    def fill_for(k, turn):
+        gap = pick(send_order, turn - 1)
+        label = lax.rem(module + gap, modules) * owned + k
+
+        @pl.loop(0, 2)
+        def _(part):
+            fill(label, part, packed.at[label], part * half)
+            bin_copy(k, 2 * gap + part).start()
+
+    def fill_own(k):
+        @pl.loop(0, 2)
+        def _(part):
+            first_row = module * per_bin + part * half
+            fill(module * owned + k, part, own.at[k], first_row)
+            pass_on(k, part)
+
+    one_results = ((2, 0, 1), (2, 4, 0), (4, 2, 0), (3, 4, 1), (4, 3, 1))
+    three_results = ((1, 3, 0),)
+
+    def coded_copies(k, stage, slot, frame):
+        pairs = ((coded, landed), (coded_peak, landed_peak))
+        return [
+            pltpu.make_async_remote_copy(
+                src_ref=source.at[stage, k],
+                dst_ref=target.at[slot, k],
+                send_sem=coded_send.at[index],
+                recv_sem=coded_recv.at[index, slot, k],
+                device_id=(frame, module),
+                device_id_type=MESH,
+            )
+            for index, (source, target) in enumerate(pairs)
+        ]
+
+    def send_coded(k, stage, result, values):
+        peak = jnp.max(values, axis=0, keepdims=True)
+        levels = values * (32767.0 / peak) + 0.5
+        coded[stage, k] = levels.astype(jnp.int32).astype(jnp.int16)
+        coded_peak[stage, k] = jnp.broadcast_to(peak * (1.0 / 32767.0), (8, frames))
+        for copy in coded_copies(k, stage, result[2], flip(result[0])):
+            copy.start()
+
+    def decode(k, slot, gap):
+        for copy in coded_copies(k, 0, slot, me):
+            copy.wait_recv()
+        values = landed[slot, k].astype(jnp.int32).astype(f32)
+        total[k, place(gap)] = values * landed_peak[slot, k, :1, :]
+
+    def direct_copy(k):
         return pltpu.make_async_remote_copy(
-            src_ref=staged.at[stage, k],
-            dst_ref=out.at[k, spot],
-            send_sem=result_send.at[stage, k],
-            recv_sem=result_recv.at[spot, k],
-            device_id=(frame, module),
-            device_id_type=MESH,
-        )
-
-    one_results = ((2, 0), (2, 4), (4, 2), (0, 2), (3, 4), (4, 3))
-    three_results = ((1, 3), (2, 1))
-
-    def result_of(k, stage, pair):
-        return result_copy(k, stage, place(pair[1] - pair[0]), flip(pair[0]))
-
-    def scale_of(block):
-        down = jnp.ones((8, gathered), jnp.bfloat16)
-        across = jnp.ones((gathered, LANES), jnp.bfloat16)
-        root = jnp.sqrt(jnp.float32(gathered))
-        row = jnp.dot(down, block, preferred_element_type=jnp.float32)[:1]
-        column = gram(block, across)
-        column = jnp.concatenate([column] * (frames // LANES), axis=1)
-        return root / column, root / row
-
-    def await_frames(k, copy):
-        for j in range(parts):
-            copy(k, j).wait_recv()
-
-    def correlate(k):
-        scales = {0: scale_of(own[k])}
-        out[k, 2] = gram(own[k], own[k]) * scales[0][0] * scales[0][1]
-        await_frames(k, near_copy)
-        near_scale = scale_of(near[k])
-        own_scale = scales[0]
-        out[k, mate - me + 2] = gram(own[k], near[k]) * own_scale[0] * near_scale[1]
+            src_ref=direct.at[k],
+            dst_ref=total.at[k, jnp.where(role < 2, place(2), place(-1))],
+            send_sem=direct_send.at[0],
+            recv_sem=direct_recv.at[k],
+            device_id=(mate, module),
+            device_id_type=MESH,
+        )
+
+    def await_frames(k, flow, target):
+        whole_copy(flow, k, own.at[k], target, mate).wait_recv()
+
+    def work(k, step):
+        if step == 0:
+            await_frames(k, 0, near.at[k])
+
+            @pl.when(is_one)
+            def _():
+                await_frames(k, 1, first.at[k])
+                send_coded(k, 0, one_results[0], gram(first[k], near[k]))
+
+            @pl.when(is_three)
+            def _():
+                await_frames(k, 1, first.at[k])
+                send_coded(k, 0, three_results[0], gram(first[k], own[k]))
+
+        if step == 1:
+
+            @pl.when(is_one)
+            def _():
+                await_frames(k, 2, second.at[k])
+                send_coded(k, 1, one_results[1], gram(first[k], second[k]))
+
+            @pl.when(is_three)
+            def _():
+                direct[k] = gram(near[k], first[k])
+                direct_copy(k).start()
+
+        if step == 2:
+
+            @pl.when(is_one & shared(k))
+            def _():
+                await_frames(k, 3, third.at[k // 2])
+                send_coded(k, 3, one_results[3], gram(third[k // 2], second[k]))
+
+            @pl.when(is_three)
+            def _():
+                total[k, place(-2)] = gram(own[k], first[k])
+
+        if step == 3:
+
+            @pl.when(is_one)
+            def _():
+                send_coded(k, 2, one_results[2], gram(second[k], first[k]))
+
+            @pl.when(is_one & shared(k))
+            def _():
+                send_coded(k, 4, one_results[4], gram(second[k], third[k // 2]))
+
+        if step == 4:
+
+            @pl.when(is_one)
+            def _():
+                direct[k] = gram(near[k], first[k])
+                direct_copy(k).start()
+                total[k, place(1)] = gram(own[k], first[k])
+
+        if step == 5:
+            total[k, mate - me + 2] = gram(own[k], near[k])
+            total[k, 2] = gram(own[k], own[k])
+
+    def finish(k):
+        @pl.when((role == 0) | is_two)
+        def _():
+            direct_copy(k).wait_recv()
+
+        @pl.when(role > 0)
+        def _():
+            decode(k, 0, 2)
+
+        @pl.when(is_two)
+        def _():
+            decode(k, 1, -2)
 
         @pl.when(is_three)
         def _():
-            await_frames(k, first_copy)
-            scale = scale_of(first[k])
-            staged[0, k] = gram(first[k], own[k]) * scale[0] * own_scale[1]
-            result_of(k, 0, three_results[0]).start()
-            staged[1, k] = gram(near[k], first[k]) * near_scale[0] * scale[1]
-            result_of(k, 1, three_results[1]).start()
-            out[k, place(-2)] = gram(own[k], first[k]) * own_scale[0] * scale[1]
-
-        @pl.when(is_one)
-        def _():
-            await_frames(k, first_copy)
-            scale = scale_of(first[k])
-            staged[0, k] = gram(first[k], near[k]) * scale[0] * near_scale[1]
-            result_of(k, 0, one_results[0]).start()
-            await_frames(k, second_copy)
-            far_scale = scale_of(second[k])
-            staged[1, k] = gram(first[k], second[k]) * scale[0] * far_scale[1]
-            result_of(k, 1, one_results[1]).start()
-            staged[2, k] = gram(second[k], first[k]) * far_scale[0] * scale[1]
-            result_of(k, 2, one_results[2]).start()
-
-            @pl.when(shared(k))
-            def _():
-                await_frames(k, third_copy)
-                block = third.at[k // 2]
-                third_scale = scale_of(block[...])
-                staged[4, k] = gram(block[...], second[k]) * third_scale[0] * far_scale[1]
-                result_of(k, 4, one_results[4]).start()
-                staged[5, k] = gram(second[k], block[...]) * far_scale[0] * third_scale[1]
-                result_of(k, 5, one_results[5]).start()
-
-            staged[3, k] = gram(near[k], first[k]) * near_scale[0] * scale[1]
-            result_of(k, 3, one_results[3]).start()
-            out[k, place(1)] = gram(own[k], first[k]) * own_scale[0] * scale[1]
-
-    @pl.loop(0, owned)
-    def _(k):
+            decode(k, 1, 1)
+
+    for k in range(2):
         @pl.loop(1, modules)
         def _(gap):
-            label = lax.rem(module + gap, modules) * owned + k
-            fill(label, packed.at[label], 0)
-            bin_copy(k, 2 * gap).start()
-            bin_copy(k, 2 * gap + 1).start()
-
-        fill(module * owned + k, own.at[k], module * per_bin)
-        pass_on(k, 0)
-        pass_on(k, 1)
+            fill_for(k, gap)
+
+        fill_own(k)
 
     @pl.when(role == 0)
     def _():
         for k in range(owned):
-            out[k, place(-1)] = jnp.zeros((frames, frames), jnp.float32)
+            total[k, place(-1)] = jnp.zeros((frames, frames), f32)
 
     @pl.when(role < 2)
     def _():
         for k in range(owned):
-            out[k, place(-2)] = jnp.zeros((frames, frames), jnp.float32)
+            total[k, place(-2)] = jnp.zeros((frames, frames), f32)
+
+    def take(k, column, part):
+        gap = modules - pick(take_order, jnp.int32(column))
+        piece = 2 * gap + part
+        bin_copy(k, piece).wait_recv()
+        pass_on(k, piece)
+
+    take(0, 0, 0)
+    take(0, 0, 1)
 
     @pl.loop(0, owned + 1)
     def _(turn_index):
-        @pl.when(turn_index < owned)
-        def _():
-            for piece in range(2, parts):
-                bin_copy(turn_index, piece).wait()
-                pass_on(turn_index, piece)
-
-        @pl.when(turn_index >= 1)
-        def _():
-            correlate(turn_index - 1)
-
-    @pl.loop(0, owned)
-    def _(k):
-        for j in range(parts):
-            near_copy(k, j).wait_send()
-
-        @pl.when(is_one | is_two)
-        def _():
-            for j in range(parts):
-                first_copy(k, j).wait_send()
-
-        @pl.when(is_three)
-        def _():
-            for j in range(parts):
-                second_copy(k, j).wait_send()
-
-        @pl.when(is_three & shared(k))
-        def _():
-            for j in range(parts):
-                third_copy(k, j).wait_send()
-
-        @pl.when(is_one)
-        def _():
-            for stage in range(4):
-                result_of(k, stage, one_results[stage]).wait_send()
-
-        @pl.when(is_one & shared(k))
-        def _():
-            for stage in range(4, 6):
-                result_of(k, stage, one_results[stage]).wait_send()
-
-        @pl.when(is_three)
-        def _():
-            for stage in range(2):
-                result_of(k, stage, three_results[stage]).wait_send()
-
-        result_copy(k, 0, place(2), me).wait_recv()
-
-        @pl.when(is_two)
-        def _():
-            result_copy(k, 0, place(-2), me).wait_recv()
-            result_copy(k, 0, place(-1), me).wait_recv()
-
-        @pl.when(is_three)
-        def _():
-            result_copy(k, 0, place(1), me).wait_recv()
-
-
-def correlate_square(order, raw_frames, dark_frame, flat_field, bins):
+        for step in range(2, parts):
+            column = step // 2 - 1
+            taken = turn_index + int(column == 0)
+
+            @pl.when(taken < owned)
+            def _():
+                take(taken, column, step % 2)
+
+            @pl.when(turn_index + 2 < owned)
+            def _():
+                if step - 1 < modules:
+                    fill_for(turn_index + 2, step - 1)
+                elif step - 1 == modules:
+                    fill_own(turn_index + 2)
+
+            @pl.when(turn_index >= 1)
+            def _():
+                work(turn_index - 1, step - 2)
+
+        @pl.when(turn_index >= 2)
+        def _():
+            finish(turn_index - 2)
+
+    finish(owned - 1)
+
+    sent = packed.at[pl.ds(0, bins - owned)]
+    pltpu.make_async_remote_copy(
+        src_ref=sent,
+        dst_ref=sent,
+        send_sem=bin_send.at[0],
+        recv_sem=bin_recv.at[0, 0],
+        device_id=(mate, module),
+        device_id_type=MESH,
+    ).wait_send()
+    whole_copy(0, 0, own, near, mate).wait_send()
+
+    def await_coded(rows):
+        for index, source in enumerate((coded, coded_peak)):
+            pltpu.make_async_remote_copy(
+                src_ref=source.at[pl.ds(0, rows)],
+                dst_ref=source.at[pl.ds(0, rows)],
+                send_sem=coded_send.at[index],
+                recv_sem=coded_recv.at[index, 0, 0],
+                device_id=(mate, module),
+                device_id_type=MESH,
+            ).wait_send()
+
+    @pl.when(is_one | is_two)
+    def _():
+        whole_copy(1, 0, own, first, mate).wait_send()
+
+    @pl.when(is_three)
+    def _():
+        whole_copy(2, 0, own, second, mate).wait_send()
+        whole_copy(3, 0, own.at[pl.ds(0, owned // 2)], third, mate).wait_send()
+        await_coded(1)
+
+    @pl.when(is_one)
+    def _():
+        await_coded(4)
+
+    @pl.when(is_one | is_three)
+    def _():
+        pltpu.make_async_remote_copy(
+            src_ref=direct,
+            dst_ref=direct,
+            send_sem=direct_send.at[0],
+            recv_sem=direct_recv.at[0],
+            device_id=(mate, module),
+            device_id_type=MESH,
+        ).wait_send()
+
+
+def correlate_square(raw_frames, dark_frame, flat_field, membership):
     frames, pixels = raw_frames.shape
+    bins = membership.shape[0]
     modules = lax.axis_size("module")
     per_bin = pixels // bins
     owned = bins // modules
@@ -808,47 +990,65 @@
     slab = 2 * per_bin
     vmem = pl.BlockSpec(memory_space=pltpu.VMEM)
     dma = pltpu.SemaphoreType.DMA
+    f32, bf16 = jnp.float32, jnp.bfloat16
     block = (owned, gathered, frames)
     return pl.pallas_call(
         functools.partial(square_kernel, modules),
-        out_shape=jax.ShapeDtypeStruct((owned, 5, frames, frames), jnp.float32),
+        out_shape=pltpu.VMEM((owned, 5, frames, frames), f32),
         in_specs=[
-            pl.BlockSpec(memory_space=pltpu.SMEM),
             pl.BlockSpec(memory_space=pl.ANY),
-            vmem,
-            vmem,
+            pl.BlockSpec(memory_space=pl.ANY),
+            pl.BlockSpec(memory_space=pl.ANY),
+            pl.BlockSpec(memory_space=pl.ANY),
         ],
         out_specs=vmem,
         scratch_shapes=[
-            pltpu.VMEM((2, frames, slab), jnp.int32),
-            pltpu.VMEM((pixels, frames), jnp.float32),
-            pltpu.VMEM((bins, per_bin, frames), jnp.bfloat16),
-            pltpu.VMEM(block, jnp.bfloat16),
-            pltpu.VMEM(block, jnp.bfloat16),
-            pltpu.VMEM(block, jnp.bfloat16),
-            pltpu.VMEM(block, jnp.bfloat16),
-            pltpu.VMEM((owned // 2, gathered, frames), jnp.bfloat16),
-            pltpu.VMEM((6, owned, frames, frames), jnp.float32),
+            pltpu.VMEM((1, pixels), f32),
+            pltpu.VMEM((1, pixels), f32),
+            pltpu.VMEM((bins, pixels), jnp.int32),
+            pltpu.VMEM((2 * pixels // LANES, pixels), bf16),
+            pltpu.VMEM((LANES, pixels), bf16),
+            pltpu.VMEM((pixels // LANES, LANES), jnp.int32),
+            pltpu.SMEM((pixels // LANES, LANES), jnp.int32),
+            pltpu.VMEM((pixels // slab, frames, slab), jnp.int32),
+            pltpu.VMEM((pixels, frames), f32),
+            pltpu.VMEM((bins, frames), f32),
+            pltpu.VMEM((modules, bins, frames), f32),
+            pltpu.VMEM((bins, per_bin, frames), bf16),
+            pltpu.VMEM(block, bf16),
+            pltpu.VMEM(block, bf16),
+            pltpu.VMEM(block, bf16),
+            pltpu.VMEM(block, bf16),
+            pltpu.VMEM((owned // 2, gathered, frames), bf16),
+            pltpu.VMEM((owned, frames, frames), f32),
+            pltpu.VMEM((5, owned, frames, frames), jnp.int16),
+            pltpu.VMEM((5, owned, 8, frames), f32),
+            pltpu.VMEM((2, owned, frames, frames), jnp.int16),
+            pltpu.VMEM((2, owned, 8, frames), f32),
+            dma((pixels // slab,)),
+            dma((4,)),
+            dma((modules - 1,)),
+            dma((modules - 1,)),
+            dma((1,)),
+            dma((owned, 2 * modules)),
+            dma((4,)),
+            dma((4, owned)),
+            dma((1,)),
+            dma((owned,)),
             dma((2,)),
-            dma((owned, 2 * modules)),
-            dma((owned, 2 * modules)),
-            dma((4, owned, 2 * modules)),
-            dma((4, owned, 2 * modules)),
-            dma((6, owned)),
-            dma((5, owned)),
+            dma((2, 2, owned)),
         ],
         compiler_params=pltpu.CompilerParams(
-            collective_id=1, has_side_effects=True, vmem_limit_bytes=VMEM_BYTES
+            collective_id=1, has_side_effects=True, vmem_limit_bytes=SQUARE_BYTES
         ),
-    )(order, raw_frames, dark_frame[None, :], flat_field[None, :])
+    )(raw_frames, dark_frame[None, :], flat_field[None, :], membership)
 
 
 def per_device(raw_frames, dark_frame, flat_field, membership):
-    order = pixel_order(membership)
     if lax.axis_size("frame") == 8:
-        bins = membership.shape[0]
-        result = correlate_square(order, raw_frames, dark_frame, flat_field, bins)
+        result = correlate_square(raw_frames, dark_frame, flat_field, membership)
     else:
+        order = pixel_order(membership)
         turned, sums = turn(raw_frames, dark_frame, flat_field, membership)
         result = correlate_chain(order, turned, sums)
     return result[:, None]

time: 149 us -> 123 us (0.83)
  the two profiles are of different devices: /device:TPU:12 before, /device:TPU:1 now
where the time goes in v2:
time: 123 us
  Pallas kernels  121 us (98%)
  local copies, waits for them, and re-layouts  2.36 us (2%)
    pallas_call x1, Pallas kernels, correlate_square(): pl.pallas_call(functools.partial(square_kernel, modules), out_shape=pltpu...  121 us

profile of v2, /device:TPU:1, one launch (start us, length us, event | category | flops | bytes accessed | tf_op | source)
XLA Modules:
  0.0 122.9 jit_solution(5040126901031470557)
XLA Ops:
  0.0 120.5 %shard_map.46 = f32[4,5,256,256]{3,2,1,0:T(8,128)S(1)} custom-call(s32[256,8192]{1,0:T(8,128)} %raw.1, f32[1,8192]{1,0:T(1,128)} %bitcast.6, f32[1,8192]{1,0:T(1,128)} %bitcast.7, s32[16,8192]{1,0:T(8,128)} %membership.1), custom_call_target="tpu_custom_call" | custom-call | tf_op jit(solution)/shard_map/pallas_call | solution.py:995
  120.5 2.4 %copy.7 = f32[4,1,5,256,256]{4,3,2,1,0:T(8,128)} copy(f32[4,1,5,256,256]{4,3,2,1,0:T(8,128)S(1)} %bitcast.5) | data formatting | bytes 10485760

commit v3 on v2

--- a/solution.py
+++ b/solution.py
@@ -12,7 +12,9 @@
 SQUARE_BYTES = 57 * 1024 * 1024
 LANES = 128
 SEND_ORDER = ((3, 2, 1), (2, 3, 0), (1, 0, 3), (0, 1, 2))
-TAKE_ORDER = ((1, 3, 2), (0, 2, 3), (3, 1, 0), (2, 0, 1))
+HEARD = ((1, 3, 2), (0, 3, 2), (3, 0, 1), (2, 0, 1))
+END_ARRIVALS = ((0, 0), (0, 1), (1, 0), (1, 1), (0, 2), (2, 0), (2, 1), (3, 0), (3, 1), (1, 2), (2, 2), (3, 2))
+MIDDLE_ARRIVALS = ((0, 0), (0, 1), (1, 0), (1, 1), (0, 2), (2, 0), (2, 1), (1, 2), (3, 1), (3, 0), (2, 2), (3, 2))
 
 
 def sort_pixels(members, lows_highs, lanes):
@@ -533,11 +535,6 @@
     parts = 2 * modules
     f32, bf16 = jnp.float32, jnp.bfloat16
 
-    send_order, take_order = SEND_ORDER, TAKE_ORDER
-    if modules != 4:
-        send_order = [[(m + gap) % modules for gap in range(1, modules)] for m in range(modules)]
-        take_order = [[(m - gap) % modules for gap in range(1, modules)] for m in range(modules)]
-
     side = me // 4
     sign = 1 - 2 * side
 
@@ -590,17 +587,15 @@
 
     fetch = pltpu.make_async_copy(membership, members, order_sem.at[0])
     fetch.start()
-    fetch_dark = pltpu.make_async_copy(dark_frame, dark, order_sem.at[2])
+    fetch_dark = pltpu.make_async_copy(dark_frame, dark, order_sem.at[1])
     fetch_dark.start()
-    fetch_flat = pltpu.make_async_copy(flat_field, flat, order_sem.at[3])
+    fetch_flat = pltpu.make_async_copy(flat_field, flat, order_sem.at[2])
     fetch_flat.start()
     sums[...] = jnp.zeros_like(sums)
+    load(0).start()
     fetch.wait()
-    for index in range(slabs):
+    for index in range(1, slabs):
         load(index).start()
-    table[...] = sort_pixels(members, lows_highs, lanes)
-    spread = pltpu.make_async_copy(table, order, order_sem.at[1])
-    spread.start()
     fetch_dark.wait()
     fetch_flat.wait()
 
@@ -632,6 +627,15 @@
     for gap in range(1, modules):
         sum_copy(gap).start()
     all_sums[module] = sums[...]
+    table[...] = sort_pixels(members, lows_highs, lanes)
+
+    def spread(line):
+        return pltpu.make_async_copy(
+            table.at[line], order.at[pl.ds(line * LANES, LANES)], order_sem.at[3 + line]
+        )
+
+    for line in range(table.shape[0]):
+        spread(line).start()
 
     @pl.loop(0, slabs)
     def _(index):
@@ -644,18 +648,18 @@
         bin_sums = bin_sums + all_sums[source]
     all_sums[0] = jnp.sqrt(f32(gathered)) / bin_sums
 
-    spread.wait()
+    for line in range(table.shape[0]):
+        spread(line).wait()
     row_index = lax.broadcasted_iota(jnp.int32, (8, frames), 0)
 
     def fill(label, part, target, first_row):
         factor = all_sums[0, pl.ds(label, 1), :]
 
         def tile(start):
-            line, lane = start // LANES, lax.rem(start, LANES)
-            lines = jnp.broadcast_to(turned[pl.ds(order[line, lane], 1), :], (8, frames))
+            lines = jnp.broadcast_to(turned[pl.ds(order[start], 1), :], (8, frames))
             for row in range(1, 8):
-                line_at = turned[pl.ds(order[line, lane + row], 1), :]
-                lines = jnp.where(row_index == row, line_at, lines)
+                line = turned[pl.ds(order[start + row], 1), :]
+                lines = jnp.where(row_index == row, line, lines)
             return lines * factor
 
         def tiles(group, carry):
@@ -744,7 +748,7 @@
         return found
 
     def fill_for(k, turn):
-        gap = pick(send_order, turn - 1)
+        gap = pick(SEND_ORDER, turn - 1)
         label = lax.rem(module + gap, modules) * owned + k
 
         @pl.loop(0, 2)
@@ -822,7 +826,7 @@
             @pl.when(is_one)
             def _():
                 await_frames(k, 2, second.at[k])
-                send_coded(k, 1, one_results[1], gram(first[k], second[k]))
+                send_coded(k, 2, one_results[2], gram(second[k], first[k]))
 
             @pl.when(is_three)
             def _():
@@ -831,24 +835,21 @@
 
         if step == 2:
 
+            @pl.when(is_one)
+            def _():
+                send_coded(k, 1, one_results[1], gram(first[k], second[k]))
+
+            @pl.when(is_three)
+            def _():
+                total[k, place(-2)] = gram(own[k], first[k])
+
+        if step == 3:
+
             @pl.when(is_one & shared(k))
             def _():
                 await_frames(k, 3, third.at[k // 2])
+                send_coded(k, 4, one_results[4], gram(second[k], third[k // 2]))
                 send_coded(k, 3, one_results[3], gram(third[k // 2], second[k]))
-
-            @pl.when(is_three)
-            def _():
-                total[k, place(-2)] = gram(own[k], first[k])
-
-        if step == 3:
-
-            @pl.when(is_one)
-            def _():
-                send_coded(k, 2, one_results[2], gram(second[k], first[k]))
-
-            @pl.when(is_one & shared(k))
-            def _():
-                send_coded(k, 4, one_results[4], gram(second[k], third[k // 2]))
 
         if step == 4:
 
@@ -879,10 +880,11 @@
         def _():
             decode(k, 1, 1)
 
-    for k in range(2):
+    @pl.loop(0, owned)
+    def _(k):
         @pl.loop(1, modules)
-        def _(gap):
-            fill_for(k, gap)
+        def _(turn):
+            fill_for(k, turn)
 
         fill_own(k)
 
@@ -896,39 +898,48 @@
         for k in range(owned):
             total[k, place(-2)] = jnp.zeros((frames, frames), f32)
 
-    def take(k, column, part):
-        gap = modules - pick(take_order, jnp.int32(column))
-        piece = 2 * gap + part
-        bin_copy(k, piece).wait_recv()
-        pass_on(k, piece)
-
-    take(0, 0, 0)
-    take(0, 0, 1)
-
-    @pl.loop(0, owned + 1)
-    def _(turn_index):
-        for step in range(2, parts):
-            column = step // 2 - 1
-            taken = turn_index + int(column == 0)
-
-            @pl.when(taken < owned)
-            def _():
-                take(taken, column, step % 2)
-
-            @pl.when(turn_index + 2 < owned)
-            def _():
-                if step - 1 < modules:
-                    fill_for(turn_index + 2, step - 1)
-                elif step - 1 == modules:
-                    fill_own(turn_index + 2)
-
-            @pl.when(turn_index >= 1)
-            def _():
-                work(turn_index - 1, step - 2)
-
-        @pl.when(turn_index >= 2)
-        def _():
-            finish(turn_index - 2)
+    at_end = (module == 0) | (module == modules - 1)
+
+    def choose(values, index):
+        found = index * 0 + values[0]
+        for spot, value in enumerate(values):
+            found = jnp.where(index == spot, value, found)
+        return found
+
+    def take(spot):
+        end_k, end_column = (choose(values, spot) for values in zip(*END_ARRIVALS))
+        middle_k, middle_column = (choose(values, spot) for values in zip(*MIDDLE_ARRIVALS))
+        k = jnp.where(at_end, end_k, middle_k)
+        gap = modules - pick(HEARD, jnp.where(at_end, end_column, middle_column))
+
+        @pl.loop(0, 2)
+        def _(part):
+            piece = 2 * gap + part
+            bin_copy(k, piece).wait_recv()
+            pass_on(k, piece)
+
+    early = 8
+
+    @pl.loop(0, early)
+    def _(spot):
+        take(spot)
+
+    @pl.loop(0, owned)
+    def _(k):
+        for stage in range(6):
+            work(k, stage)
+
+        @pl.when(k < owned - 1)
+        def _():
+            take(early + k + jnp.minimum(k, 1))
+
+        @pl.when(k == 0)
+        def _():
+            take(early + 1 + k)
+
+        @pl.when(k >= 1)
+        def _():
+            finish(k - 1)
 
     finish(owned - 1)
 
@@ -1009,7 +1020,7 @@
             pltpu.VMEM((2 * pixels // LANES, pixels), bf16),
             pltpu.VMEM((LANES, pixels), bf16),
             pltpu.VMEM((pixels // LANES, LANES), jnp.int32),
-            pltpu.SMEM((pixels // LANES, LANES), jnp.int32),
+            pltpu.SMEM((pixels,), jnp.int32),
             pltpu.VMEM((pixels // slab, frames, slab), jnp.int32),
             pltpu.VMEM((pixels, frames), f32),
             pltpu.VMEM((bins, frames), f32),
@@ -1026,7 +1037,7 @@
             pltpu.VMEM((2, owned, frames, frames), jnp.int16),
             pltpu.VMEM((2, owned, 8, frames), f32),
             dma((pixels // slab,)),
-            dma((4,)),
+            dma((3 + pixels // LANES,)),
             dma((modules - 1,)),
             dma((modules - 1,)),
             dma((1,)),
@@ -1045,7 +1056,8 @@
 
 
 def per_device(raw_frames, dark_frame, flat_field, membership):
-    if lax.axis_size("frame") == 8:
+    square = lax.axis_size("frame") == 8 and lax.axis_size("module") == 4
+    if square and membership.shape[0] == 16:
         result = correlate_square(raw_frames, dark_frame, flat_field, membership)
     else:
         order = pixel_order(membership)

time: 123 us -> 119 us (0.967)
  the two profiles are of different devices: /device:TPU:1 before, /device:TPU:4 now
where the time goes in v3:
time: 119 us
  Pallas kernels  117 us (98%)
  local copies, waits for them, and re-layouts  2.36 us (2%)
    pallas_call x1, Pallas kernels, correlate_square(): pl.pallas_call(functools.partial(square_kernel, modules), out_shape=pltpu...  117 us

profile of v3, /device:TPU:4, one launch (start us, length us, event | category | flops | bytes accessed | tf_op | source)
XLA Modules:
  0.0 119.3 jit_solution(4463153432603624060)
XLA Ops:
  0.0 116.9 %shard_map.46 = f32[4,5,256,256]{3,2,1,0:T(8,128)S(1)} custom-call(s32[256,8192]{1,0:T(8,128)} %raw.1, f32[1,8192]{1,0:T(1,128)} %bitcast.6, f32[1,8192]{1,0:T(1,128)} %bitcast.7, s32[16,8192]{1,0:T(8,128)} %membership.1), custom_call_target="tpu_custom_call" | custom-call | tf_op jit(solution)/shard_map/pallas_call | solution.py:1006
  117.0 2.4 %copy.7 = f32[4,1,5,256,256]{4,3,2,1,0:T(8,128)} copy(f32[4,1,5,256,256]{4,3,2,1,0:T(8,128)S(1)} %bitcast.5) | data formatting | bytes 10485760

commit v4 on v3

--- a/solution.py
+++ b/solution.py
@@ -11,13 +11,16 @@
 VMEM_BYTES = 60 * 1024 * 1024
 SQUARE_BYTES = 57 * 1024 * 1024
 LANES = 128
+PIECES = 4
 SEND_ORDER = ((3, 2, 1), (2, 3, 0), (1, 0, 3), (0, 1, 2))
+LATE_ORDER = ((3, 2, 1), (3, 2, 0), (0, 1, 3), (0, 1, 2))
+LATE = 3
 HEARD = ((1, 3, 2), (0, 3, 2), (3, 0, 1), (2, 0, 1))
 END_ARRIVALS = ((0, 0), (0, 1), (1, 0), (1, 1), (0, 2), (2, 0), (2, 1), (3, 0), (3, 1), (1, 2), (2, 2), (3, 2))
 MIDDLE_ARRIVALS = ((0, 0), (0, 1), (1, 0), (1, 1), (0, 2), (2, 0), (2, 1), (1, 2), (3, 1), (3, 0), (2, 2), (3, 2))
 
 
-def sort_pixels(members, lows_highs, lanes):
+def place_pixels(members, lows_highs, lanes, chunks, base):
     bins, pixels = members.shape
     per_bin = pixels // bins
     span = 2 * LANES
@@ -26,11 +29,12 @@
     shape = (span, span + LANES)
     upto = lax.broadcasted_iota(jnp.int32, shape, 0) <= lax.broadcasted_iota(jnp.int32, shape, 1)
     upto = upto.astype(f32).astype(bf16)
-    base = lax.broadcasted_iota(jnp.int32, (bins, span), 0).astype(f32) * per_bin - 1.0
+    if base is None:
+        base = lax.broadcasted_iota(jnp.int32, (bins, span), 0).astype(f32) * per_bin - 1.0
     row_of = lax.broadcasted_iota(jnp.int32, (rows, span), 0)
     lane_of = lax.broadcasted_iota(jnp.int32, (LANES, span), 0)
     place = lax.broadcasted_iota(jnp.int32, (rows, span), 1).astype(f32)
-    for chunk in range(pixels // span):
+    for chunk in chunks:
         columns = slice(chunk * span, (chunk + 1) * span)
         one_hot = members[:, columns].astype(f32)
         seen = jnp.dot(one_hot.astype(bf16), upto, preferred_element_type=f32)
@@ -42,14 +46,23 @@
         lanes[:, columns] = in_lane.astype(f32).astype(bf16)
         lows_highs[:rows, columns] = jnp.where(in_row, place, 0.0).astype(bf16)
         lows_highs[rows:, columns] = jnp.where(in_row, float(chunk), 0.0).astype(bf16)
+    return base
+
+
+def order_table(lows_highs, lanes):
+    rows, pixels = lows_highs.shape[0] // 2, lows_highs.shape[1]
     both = (((1,), (1,)), ((), ()))
-    table = lax.dot_general(lows_highs[...], lanes[...], both, preferred_element_type=f32)
-    table = (table[rows:] * span + table[:rows]).astype(jnp.int32)
+    table = lax.dot_general(
+        lows_highs[...], lanes[...], both, preferred_element_type=jnp.float32
+    )
+    table = (table[rows:] * (2 * LANES) + table[:rows]).astype(jnp.int32)
     return jnp.clip(table, 0, pixels - 1)
 
 
 def order_kernel(members, order, lows_highs, lanes):
-    order[...] = sort_pixels(members, lows_highs, lanes)
+    chunks = range(members.shape[1] // (2 * LANES))
+    place_pixels(members, lows_highs, lanes, chunks, None)
+    order[...] = order_table(lows_highs, lanes)
 
 
 def pixel_order(membership):
@@ -531,8 +544,7 @@
     per_bin = pixels // bins
     owned = bins // modules
     gathered = per_bin * modules
-    half = per_bin // 2
-    parts = 2 * modules
+    share = per_bin // PIECES
     f32, bf16 = jnp.float32, jnp.bfloat16
 
     side = me // 4
@@ -596,6 +608,8 @@
     fetch.wait()
     for index in range(1, slabs):
         load(index).start()
+    chunks = pixels // (2 * LANES)
+    base = place_pixels(members, lows_highs, lanes, range(chunks // 2), None)
     fetch_dark.wait()
     fetch_flat.wait()
 
@@ -627,7 +641,8 @@
     for gap in range(1, modules):
         sum_copy(gap).start()
     all_sums[module] = sums[...]
-    table[...] = sort_pixels(members, lows_highs, lanes)
+    place_pixels(members, lows_highs, lanes, range(chunks // 2, chunks), base)
+    table[...] = order_table(lows_highs, lanes)
 
     def spread(line):
         return pltpu.make_async_copy(
@@ -663,22 +678,22 @@
             return lines * factor
 
         def tiles(group, carry):
-            start = label * per_bin + part * half + group * 16
+            start = label * per_bin + part * share + group * 16
             both = jnp.concatenate([tile(start), tile(start + 8)], axis=0)
             rows = pl.ds(pl.multiple_of(first_row + group * 16, 16), 16)
             target[rows, :] = both.astype(bf16)
             return carry
 
-        lax.fori_loop(0, half // 16, tiles, 0, unroll=4)
+        lax.fori_loop(0, share // 16, tiles, 0, unroll=4)
 
     def bin_copy(k, piece):
-        gap, part = piece // 2, lax.rem(piece, 2)
+        gap, part = piece // PIECES, lax.rem(piece, PIECES)
         owner = lax.rem(module + gap, modules)
-        start = pl.multiple_of(part * half, half)
-        landing = pl.multiple_of(module * per_bin + part * half, half)
+        start = pl.multiple_of(part * share, share)
+        landing = pl.multiple_of(module * per_bin + part * share, share)
         return pltpu.make_async_remote_copy(
-            src_ref=packed.at[owner * owned + k, pl.ds(start, half), :],
-            dst_ref=own.at[k, pl.ds(landing, half), :],
+            src_ref=packed.at[owner * owned + k, pl.ds(start, share), :],
+            dst_ref=own.at[k, pl.ds(landing, share), :],
             send_sem=bin_send.at[0],
             recv_sem=bin_recv.at[k, piece],
             device_id=(me, owner),
@@ -686,8 +701,9 @@
         )
 
     def rows_of(j):
-        source = lax.rem(module + modules - j // 2, modules)
-        return pl.ds(pl.multiple_of(source * per_bin + lax.rem(j, 2) * half, half), half)
+        source = lax.rem(module + modules - j // PIECES, modules)
+        start = source * per_bin + lax.rem(j, PIECES) * share
+        return pl.ds(pl.multiple_of(start, share), share)
 
     def frame_copy(flow, k, j, target, frame):
         return pltpu.make_async_remote_copy(
@@ -748,18 +764,18 @@
         return found
 
     def fill_for(k, turn):
-        gap = pick(SEND_ORDER, turn - 1)
+        gap = jnp.where(k < LATE, pick(SEND_ORDER, turn - 1), pick(LATE_ORDER, turn - 1))
         label = lax.rem(module + gap, modules) * owned + k
 
-        @pl.loop(0, 2)
+        @pl.loop(0, PIECES)
         def _(part):
-            fill(label, part, packed.at[label], part * half)
-            bin_copy(k, 2 * gap + part).start()
+            fill(label, part, packed.at[label], part * share)
+            bin_copy(k, PIECES * gap + part).start()
 
     def fill_own(k):
-        @pl.loop(0, 2)
+        @pl.loop(0, PIECES)
         def _(part):
-            first_row = module * per_bin + part * half
+            first_row = module * per_bin + part * share
             fill(module * owned + k, part, own.at[k], first_row)
             pass_on(k, part)
 
@@ -912,9 +928,9 @@
         k = jnp.where(at_end, end_k, middle_k)
         gap = modules - pick(HEARD, jnp.where(at_end, end_column, middle_column))
 
-        @pl.loop(0, 2)
+        @pl.loop(0, PIECES)
         def _(part):
-            piece = 2 * gap + part
+            piece = PIECES * gap + part
             bin_copy(k, piece).wait_recv()
             pass_on(k, piece)
 
@@ -1041,7 +1057,7 @@
             dma((modules - 1,)),
             dma((modules - 1,)),
             dma((1,)),
-            dma((owned, 2 * modules)),
+            dma((owned, PIECES * modules)),
             dma((4,)),
             dma((4, owned)),
             dma((1,)),

time: 119 us -> 116 us (0.975)
  the two profiles are of different devices: /device:TPU:4 before, /device:TPU:12 now
where the time goes in v4:
time: 116 us
  Pallas kernels  114 us (98%)
  local copies, waits for them, and re-layouts  2.36 us (2%)
    pallas_call x1, Pallas kernels, correlate_square(): pl.pallas_call(functools.partial(square_kernel, modules), out_shape=pltpu...  114 us
    unnamed x1, local copies, waits for them, and re-layouts  2.36 us

profile of v4, /device:TPU:12, one launch (start us, length us, event | category | flops | bytes accessed | tf_op | source)
XLA Modules:
  0.0 116.1 jit_solution(2070517204707691716)
XLA Ops:
  0.0 113.8 %shard_map.46 = f32[4,5,256,256]{3,2,1,0:T(8,128)S(1)} custom-call(s32[256,8192]{1,0:T(8,128)} %raw.1, f32[1,8192]{1,0:T(1,128)} %bitcast.6, f32[1,8192]{1,0:T(1,128)} %bitcast.7, s32[16,8192]{1,0:T(8,128)} %membership.1), custom_call_target="tpu_custom_call" | custom-call | tf_op jit(solution)/shard_map/pallas_call | solution.py:1022
  113.8 2.4 %copy.7 = f32[4,1,5,256,256]{4,3,2,1,0:T(8,128)} copy(f32[4,1,5,256,256]{4,3,2,1,0:T(8,128)S(1)} %bitcast.5) | data formatting | bytes 10485760

commit v5 on v4

--- a/solution.py
+++ b/solution.py
@@ -652,8 +652,7 @@
     for line in range(table.shape[0]):
         spread(line).start()
 
-    @pl.loop(0, slabs)
-    def _(index):
+    for index in range(slabs):
         turned[columns_of(index), :] = intensity(index).T
 
     for gap in range(1, modules):

time: 116 us -> 115 us (level)
  Pallas kernels: 114 us -> 112 us
    pallas_call x1, Pallas kernels: 114 us -> 112 us  [correlate_square(): pl.pallas_call(functools.partial(square_kernel, modules), out_shape=pltpu...]
where the time goes in v5:
time: 115 us
  Pallas kernels  112 us (97%)
  local copies, waits for them, and re-layouts  2.36 us (2%)
    pallas_call x1, Pallas kernels, correlate_square(): pl.pallas_call(functools.partial(square_kernel, modules), out_shape=pltpu...  112 us
    unnamed x1, local copies, waits for them, and re-layouts  2.36 us

profile of v5, /device:TPU:12, one launch (start us, length us, event | category | flops | bytes accessed | tf_op | source)
XLA Modules:
  0.0 114.7 jit_solution(15630191758472686581)
XLA Ops:
  0.0 112.3 %shard_map.46 = f32[4,5,256,256]{3,2,1,0:T(8,128)S(1)} custom-call(s32[256,8192]{1,0:T(8,128)} %raw.1, f32[1,8192]{1,0:T(1,128)} %bitcast.6, f32[1,8192]{1,0:T(1,128)} %bitcast.7, s32[16,8192]{1,0:T(8,128)} %membership.1), custom_call_target="tpu_custom_call" | custom-call | tf_op jit(solution)/shard_map/pallas_call | solution.py:1021
  112.3 2.4 %copy.7 = f32[4,1,5,256,256]{4,3,2,1,0:T(8,128)} copy(f32[4,1,5,256,256]{4,3,2,1,0:T(8,128)S(1)} %bitcast.5) | data formatting | bytes 10485760

commit v6 on v5

--- a/solution.py
+++ b/solution.py
@@ -11,7 +11,7 @@
 VMEM_BYTES = 60 * 1024 * 1024
 SQUARE_BYTES = 57 * 1024 * 1024
 LANES = 128
-PIECES = 4
+PIECES = 8
 SEND_ORDER = ((3, 2, 1), (2, 3, 0), (1, 0, 3), (0, 1, 2))
 LATE_ORDER = ((3, 2, 1), (3, 2, 0), (0, 1, 3), (0, 1, 2))
 LATE = 3

time: 115 us -> 115 us (level)
  no operation moved by 1% of the time
where the time goes in v6:
time: 115 us
  Pallas kernels  113 us (98%)
  local copies, waits for them, and re-layouts  2.36 us (2%)
    pallas_call x1, Pallas kernels, correlate_square(): pl.pallas_call(functools.partial(square_kernel, modules), out_shape=pltpu...  113 us
    unnamed x1, local copies, waits for them, and re-layouts  2.36 us

profile of v6, /device:TPU:12, one launch (start us, length us, event | category | flops | bytes accessed | tf_op | source)
XLA Modules:
  0.0 115.0 jit_solution(914700167820510904)
XLA Ops:
  0.0 112.7 %shard_map.46 = f32[4,5,256,256]{3,2,1,0:T(8,128)S(1)} custom-call(s32[256,8192]{1,0:T(8,128)} %raw.1, f32[1,8192]{1,0:T(1,128)} %bitcast.6, f32[1,8192]{1,0:T(1,128)} %bitcast.7, s32[16,8192]{1,0:T(8,128)} %membership.1), custom_call_target="tpu_custom_call" | custom-call | tf_op jit(solution)/shard_map/pallas_call | solution.py:1021
  112.7 2.4 %copy.7 = f32[4,1,5,256,256]{4,3,2,1,0:T(8,128)} copy(f32[4,1,5,256,256]{4,3,2,1,0:T(8,128)S(1)} %bitcast.5) | data formatting | bytes 10485760
